TPU v7x, 32 devices: a whole 2x2x4 slice. The times are simulated.
32 devices in a mesh: expert: 8 (over z, x), pair: 2 (over core), dp: 2 (over y).
Axes of the slice: x: 2, y: 2, z: 4, core: 2. Of those that a mesh axis runs over, the one named last changes fastest.
Arguments:
- tokens: bfloat16 [128, 196, 768], P(('expert', 'pair', 'dp')), may hold values from -96 to 96
- phi: bfloat16 [768, 16], replicated, may hold values from -0.25 to 0.25
- w_in: bfloat16 [8, 768, 3072], P('expert', None, 'pair'), may hold values from -0.21875 to 0.21875
- w_out: bfloat16 [8, 3072, 768], P('expert', 'pair'), may hold values from -0.109375 to 0.109375
- slot_out: bfloat16 [128, 16, 768], P(('expert', 'pair', 'dp')), may hold values from -6 to 6
- grad_out: bfloat16 [128, 196, 768], P(('expert', 'pair', 'dp')), may hold values from -6 to 6
Outputs:
- token_grad: bfloat16 [128, 196, 768], P(('expert', 'pair', 'dp'))
- phi_grad: float32 [768, 16], replicated
- grad_w_in: bfloat16 [8, 768, 3072], P('expert', 'dp', 'pair')
- grad_w_out: bfloat16 [8, 3072, 768], P('expert', 'pair', 'dp')
All inputs are finite; a program needn't handle non-finite values.
Results may differ from a plain program's by a relative error of at most 0.0086.
Values may be sent and summed in bfloat16 or wider, within the bound.
A program may use at most 128 MiB of HBM per device.

v0:
```python
import jax
import jax.numpy as jnp
from jax import lax
from jax.sharding import PartitionSpec as P


def expert_rows(z_rows, g_rows, w_first, w_second):
    pre = jnp.dot(z_rows, w_first, preferred_element_type=jnp.float32)
    act_full, gelu_back = jax.vjp(jax.nn.gelu, pre)
    act = act_full.astype(jnp.bfloat16)
    dact = lax.dot_general(
        g_rows, w_second, (((1,), (1,)), ((), ())), preferred_element_type=jnp.float32
    )
    dpre = gelu_back(dact)[0].astype(jnp.bfloat16)
    grad_second = lax.dot_general(
        act, g_rows, (((0,), (0,)), ((), ())), preferred_element_type=jnp.float32
    )
    grad_first = lax.dot_general(
        z_rows, dpre, (((0,), (0,)), ((), ())), preferred_element_type=jnp.float32
    )
    back = lax.dot_general(
        dpre, w_first, (((1,), (1,)), ((), ())), preferred_element_type=jnp.float32
    )
    return (grad_first, grad_second, back)


def local(tokens, phi, w_in, w_out, slot_out, grad_out):
    f32 = jnp.float32
    images, _, width = tokens.shape
    groups = lax.axis_size("expert")
    per_group = phi.shape[1] // groups
    experts_here = w_in.shape[0]
    slots = per_group // experts_here
    logits = jnp.einsum("bmd,ds->bms", tokens, phi, preferred_element_type=f32)
    dispatch = jax.nn.softmax(logits, axis=1)
    combine = jax.nn.softmax(logits, axis=2)
    dispatch_low = dispatch.astype(jnp.bfloat16)
    combine_low = combine.astype(jnp.bfloat16)
    slot_in = jnp.einsum("bms,bmd->bsd", dispatch_low, tokens, preferred_element_type=f32).astype(
        jnp.bfloat16
    )
    slot_grad = jnp.einsum(
        "bms,bmd->bsd", combine_low, grad_out, preferred_element_type=f32
    ).astype(jnp.bfloat16)
    outgoing_in = slot_in.reshape(images, groups, per_group, width)
    outgoing_grad = slot_grad.reshape(images, groups, per_group, width)
    arrived_in, arrived_grad = (
        lax.all_to_all(outgoing_in, "expert", split_axis=1, concat_axis=0, tiled=True),
        lax.all_to_all(outgoing_grad, "expert", split_axis=1, concat_axis=0, tiled=True),
    )
    rows_in, rows_grad = (
        lax.all_gather(arrived_in, "pair", axis=0, tiled=True),
        lax.all_gather(arrived_grad, "pair", axis=0, tiled=True),
    )
    count = rows_in.shape[0]
    z_rows = rows_in[:, 0].reshape(count * slots, width)
    g_rows = rows_grad[:, 0].reshape(count * slots, width)
    grad_first, grad_second, back = expert_rows(z_rows, g_rows, w_in[0], w_out[0])
    firsts = [grad_first]
    seconds = [grad_second]
    backs = back.reshape(count, 1, slots, width)
    back_sum = lax.psum_scatter(backs, "pair", scatter_dimension=0, tiled=True)
    grad_w_in = lax.psum_scatter(
        jnp.stack(firsts).astype(jnp.bfloat16), "dp", scatter_dimension=1, tiled=True
    )
    grad_w_out = lax.psum_scatter(
        jnp.stack(seconds).astype(jnp.bfloat16), "dp", scatter_dimension=2, tiled=True
    )
    back_low = back_sum.astype(jnp.bfloat16)
    returned = lax.all_to_all(back_low, "expert", split_axis=0, concat_axis=1, tiled=True)
    slot_in_grad = returned.reshape(images, groups * per_group, width)
    dispatch_grad = jnp.einsum("bmd,bsd->bms", tokens, slot_in_grad, preferred_element_type=f32)
    combine_grad = jnp.einsum("bmd,bsd->bms", grad_out, slot_out, preferred_element_type=f32)
    logit_grad = dispatch * (
        dispatch_grad - jnp.sum(dispatch * dispatch_grad, axis=1, keepdims=True)
    )
    logit_grad = logit_grad + combine * (
        combine_grad - jnp.sum(combine * combine_grad, axis=2, keepdims=True)
    )
    logit_low = logit_grad.astype(jnp.bfloat16)
    token_part = jnp.einsum("bms,bsd->bmd", dispatch_low, slot_in_grad, preferred_element_type=f32)
    token_grad = (
        token_part + jnp.einsum("bms,ds->bmd", logit_low, phi, preferred_element_type=f32)
    ).astype(jnp.bfloat16)
    phi_part = jnp.einsum("bmd,bms->ds", tokens, logit_low, preferred_element_type=f32)
    phi_grad = lax.psum(phi_part, ("expert", "pair", "dp"))
    return (token_grad, phi_grad, grad_w_in, grad_w_out)


def solution(mesh):
    in_specs = (
        P(("expert", "pair", "dp"), None, None),
        P(),
        P("expert", None, "pair"),
        P("expert", "pair", None),
        P(("expert", "pair", "dp"), None, None),
        P(("expert", "pair", "dp"), None, None),
    )
    out_specs = (
        P(("expert", "pair", "dp"), None, None),
        P(),
        P("expert", "dp", "pair"),
        P("expert", "pair", "dp"),
    )
    return jax.shard_map(local, mesh=mesh, in_specs=in_specs, out_specs=out_specs, check_vma=False)
```

profile of v0, /device:TPU:0, one launch (start us, length us, event | category | flops | bytes accessed | tf_op | source)
XLA Modules:
  0.0 153.0 jit_solution(3510893113097627227)
XLA Ops:
  7.2 1.8 %fusion.32 = f32[4,196,16]{1,2,0:T(8,128)S(1)} fusion(bf16[4,196,768]{2,0,1:T(4,128)(2,1)} %param.6, bf16[768,16]{0,1:T(8,128)(2,1)} %param.7), kind=kOutput, calls=%fused_computation.41 | convolution fusion | flops 19267584 | bytes 1278976 | tf_op jit(solution)/shard_map/bmd,ds->bms/dot_general | solution.py:34
  9.0 0.7 fusion.64
  9.7 1.6 %convolution_convert_fusion.3 = bf16[4,16,768]{2,1,0:T(8,128)(2,1)S(1)} fusion(bf16[4,196,768]{2,0,1:T(4,128)(2,1)} %param.11, f32[4,196]{1,0:T(4,128)S(1)} %get-tuple-element.16, f32[4,196,16]{1,2,0:T(8,128)S(1)} %fusion.32), kind=kOutput, calls=%fused_computation.19 | convolution fusion | flops 19355168 | bytes 1355840 | tf_op jit(solution)/shard_map/bms,bmd->bsd/dot_general | solution.py:42
  11.4 0.7 copy.32
  12.1 7.3 %all-to-all-start = ((bf16[4,8,2,768]{3,2,0,1:T(2,128)(2,1)}), bf16[4,8,2,768]{3,2,0,1:T(2,128)(2,1)S(1)}, u32[]{:S(2)}, u32[]{:S(2)}) async-start(bf16[4,8,2,768]{3,2,0,1:T(2,128)(2,1)} %copy.32), calls=%async_computation | async-start | bytes 196608 | tf_op jit(solution)/shard_map/all_to_all | solution.py:49
  19.3 0.7 fusion.65
  20.1 1.6 %convolution_convert_fusion.2 = bf16[4,16,768]{2,1,0:T(8,128)(2,1)S(1)} fusion(bf16[4,196,768]{2,0,1:T(4,128)(2,1)} %param.6, f32[4,16]{1,0:T(4,128)S(1)} %get-tuple-element.18, f32[4,196,16]{1,2,0:T(8,128)S(1)} %fusion.32), kind=kOutput, calls=%fused_computation.18 | convolution fusion | flops 19354628 | bytes 1352960 | tf_op jit(solution)/shard_map/bms,bmd->bsd/dot_general | solution.py:39
  21.7 0.7 copy.35
  22.4 4.0 %all-to-all-done = bf16[4,8,2,768]{3,2,0,1:T(2,128)(2,1)S(1)} async-done(((bf16[4,8,2,768]{3,2,0,1:T(2,128)(2,1)}), bf16[4,8,2,768]{3,2,0,1:T(2,128)(2,1)S(1)}, u32[]{:S(2)}, u32[]{:S(2)}) %all-to-all-start) | async-done | bytes 98336 | tf_op jit(solution)/shard_map/all_to_all | solution.py:49
  26.5 3.4 %all-to-all-start.1 = ((bf16[4,8,2,768]{3,2,0,1:T(2,128)(2,1)}), bf16[4,8,2,768]{3,2,0,1:T(2,128)(2,1)S(1)}, u32[]{:S(2)}, u32[]{:S(2)}) async-start(bf16[4,8,2,768]{3,2,0,1:T(2,128)(2,1)} %copy.35), calls=%async_computation.1 | async-start | bytes 196608 | tf_op jit(solution)/shard_map/all_to_all | solution.py:48
  29.8 0.0 reduce-scatter.6.cloned.1.call-start
  29.9 1.9 %all_gather.6 = bf16[64,1,2,768]{3,2,1,0:T(2,128)(2,1)S(1)} all-gather(bf16[32,1,2,768]{3,2,1,0:T(2,128)(2,1)S(1)} %bitcast.73), channel_id=1, replica_groups=mesh['expert'=8,'pair'=2,'dp'=2] {'pair'}, dimensions={0}, use_global_device_ids=true | all-gather | bytes 294912 | tf_op jit(solution)/shard_map/all_gather | solution.py:53
  31.8 0.1 reshape_squeeze.6
  31.9 5.0 %all-to-all-done.1 = bf16[4,8,2,768]{3,2,0,1:T(2,128)(2,1)S(1)} async-done(((bf16[4,8,2,768]{3,2,0,1:T(2,128)(2,1)}), bf16[4,8,2,768]{3,2,0,1:T(2,128)(2,1)S(1)}, u32[]{:S(2)}, u32[]{:S(2)}) %all-to-all-start.1) | async-done | bytes 98336 | tf_op jit(solution)/shard_map/all_to_all | solution.py:48
  36.9 1.9 %all_gather.7 = bf16[64,1,2,768]{3,2,1,0:T(2,128)(2,1)S(1)} all-gather(bf16[32,1,2,768]{3,2,1,0:T(2,128)(2,1)S(1)} %bitcast.74), channel_id=1, replica_groups=mesh['expert'=8,'pair'=2,'dp'=2] {'pair'}, dimensions={0}, use_global_device_ids=true | all-gather | bytes 294912 | tf_op jit(solution)/shard_map/all_gather | solution.py:52
  38.8 0.1 reshape_squeeze.7
  38.9 0.5 fusion.8
  39.4 1.2 copy-done.7
  40.6 1.8 %fusion.40 = bf16[128,1536]{1,0:T(8,128)(2,1)} fusion(f32[128,1536]{1,0:T(8,128)S(1)} %fusion.8, bf16[128,768]{1,0:T(8,128)(2,1)S(1)} %reshape_squeeze.6, bf16[1,1536,768]{2,1,0:T(8,128)(2,1)S(1)} %copy-done.7), kind=kOutput, calls=%fused_computation.49 | convolution fusion | flops 305922048 | bytes 3735552 | tf_op jit(solution)/shard_map/dot_general | solution.py:11
  42.4 1.9 %reshape.35 = bf16[64,2,1536]{2,1,0:T(2,128)(2,1)} reshape(bf16[128,1536]{1,0:T(8,128)(2,1)} %fusion.40) | data formatting | bytes 786432 | tf_op jit(solution)/shard_map/reshape.16
  44.3 2.6 %fusion.12 = f32[64,1,2,768]{3,0,2,1:T(8,128)} fusion(bf16[1,768,1536]{2,1,0:T(8,128)(2,1)S(1)} %copy-done, bf16[64,2,1536]{2,1,0:T(2,128)(2,1)} %reshape.35), kind=kOutput, calls=%fused_computation.17 | convolution fusion | flops 301989888 | bytes 3145728 | tf_op jit(solution)/shard_map/dot_general | solution.py:21
  46.9 0.0 reduce-scatter.6.cloned.1.call-update
  46.9 0.0 reduce-scatter.10.cloned.1.call-start
  47.0 2.3 %fusion.5 = bf16[1,1536,768]{2,1,0:T(8,128)(2,1)} fusion(bf16[128,768]{1,0:T(8,128)(2,1)S(1)} %reshape_squeeze.6, f32[128,1536]{1,0:T(8,128)S(1)} %fusion.8), kind=kOutput, calls=%fused_computation.7 | convolution fusion | flops 304939008 | bytes 3342336 | tf_op jit(solution)/shard_map/dot_general | solution.py:15
  49.3 12.2 %copy.44 = bf16[1,1536,768]{1,0,2:T(2,128)(2,1)} copy(bf16[1,1536,768]{2,1,0:T(8,128)(2,1)} %fusion.5) | data formatting | bytes 4718592
  61.5 4.4 %copy.63 = bf16[768,1,1536]{2,0,1:T(8,128)(2,1)} copy(bf16[768,1,1536]{2,1,0:T(2,128)(2,1)} %bitcast.69) | data formatting | bytes 4718592
  65.8 0.0 reduce-scatter.10.cloned.1.call-update
  65.9 0.0 reduce-scatter.8.cloned.1.call-start
  65.9 0.9 copy-done.1
  66.8 2.2 %fusion.4 = bf16[1,768,1536]{2,1,0:T(8,128)(2,1)} fusion(bf16[128,768]{1,0:T(8,128)(2,1)S(1)} %reshape_squeeze.7, bf16[128,1536]{1,0:T(8,128)(2,1)S(1)} %copy-done.1), kind=kOutput, calls=%fused_computation.6 | convolution fusion | flops 303169536 | bytes 2949120 | tf_op jit(solution)/shard_map/dot_general | solution.py:18
  69.1 0.0 reduce-scatter.8.cloned.1.call-update
  69.1 0.9 copy-done.8
  70.0 1.8 %fusion.25 = f32[4,196,16]{1,2,0:T(8,128)S(1)} fusion(bf16[4,16,768]{2,1,0:T(8,128)(2,1)S(1)} %copy-done.8, bf16[4,196,768]{2,0,1:T(4,128)(2,1)} %param.11), kind=kOutput, calls=%fused_computation.34 | convolution fusion | flops 19267584 | bytes 1352704 | tf_op jit(solution)/shard_map/bmd,bsd->bms/dot_general | solution.py:73
  71.8 1.0 convert_element_type.44
  72.8 0.7 copy.38
  73.5 3.5 %all-to-all-start.2 = ((bf16[32,1,2,768]{3,2,1,0:T(2,128)(2,1)}), bf16[32,1,2,768]{3,2,1,0:T(2,128)(2,1)S(1)}, u32[]{:S(2)}, u32[]{:S(2)}) async-start(bf16[32,1,2,768]{3,2,1,0:T(2,128)(2,1)} %copy.38), calls=%async_computation.3 | async-start | bytes 196608 | tf_op jit(solution)/shard_map/all_to_all | solution.py:70
  77.1 0.2 fusion.23
  77.3 6.8 %all-to-all-done.2 = bf16[32,1,2,768]{3,2,1,0:T(2,128)(2,1)S(1)} async-done(((bf16[32,1,2,768]{3,2,1,0:T(2,128)(2,1)}), bf16[32,1,2,768]{3,2,1,0:T(2,128)(2,1)S(1)}, u32[]{:S(2)}, u32[]{:S(2)}) %all-to-all-start.2) | async-done | bytes 98336 | tf_op jit(solution)/shard_map/all_to_all | solution.py:70
  84.1 0.1 copy.64
  84.3 1.7 %convolution_bitcast_fusion = f32[4,196,16]{1,2,0:T(8,128)S(1)} fusion(bf16[4,16,768]{2,1,0:T(8,128)(2,1)S(1)} %reshape.36, bf16[4,196,768]{2,0,1:T(4,128)(2,1)} %param.6), kind=kOutput, calls=%fused_computation.24 | convolution fusion | flops 19267584 | bytes 1352704 | tf_op jit(solution)/shard_map/bmd,bsd->bms/dot_general | solution.py:72
  85.9 0.0 copy-start.3
  86.0 2.2 %fusion.28 = f32[4,196,768]{2,1,0:T(8,128)} fusion(f32[4,196,16]{1,2,0:T(8,128)S(1)} %fusion.23, f32[4,196,16]{1,2,0:T(8,128)S(1)} %convolution_bitcast_fusion, bf16[768,16]{0,1:T(8,128)(2,1)S(1)} %copy-done.6, f32[4,196,16]{1,2,0:T(8,128)S(1)} %copy-done.4, f32[4,16]{1,0:T(4,128)S(1)} %get-tuple-element.18), kind=kOutput, calls=%fused_computation.37 | convolution fusion | flops 19355652 | bytes 2583808 | tf_op jit(solution)/shard_map/bms,ds->bmd/dot_general | solution.py:83
  88.1 3.6 %add_convert_fusion = bf16[4,196,768]{2,1,0:T(8,128)(2,1)} fusion(f32[4,196,768]{2,1,0:T(8,128)} %fusion.28, bf16[4,16,768]{2,1,0:T(8,128)(2,1)S(1)} %reshape.36, f32[4,16]{1,0:T(4,128)S(1)} %get-tuple-element.18, f32[4,196,16]{1,2,0:T(8,128)S(1)} %copy-done.3), kind=kOutput, calls=%fused_computation.8 | convolution fusion | flops 20509700 | bytes 3761408 | tf_op jit(solution)/shard_map/bms,bsd->bmd/dot_general | solution.py:81
  91.7 2.8 %copy.43 = bf16[4,196,768]{2,0,1:T(4,128)(2,1)} copy(bf16[4,196,768]{2,1,0:T(8,128)(2,1)} %add_convert_fusion) | data formatting | bytes 2408448
  94.6 1.7 %convolution_bitcast_fusion.1 = f32[768,16]{0,1:T(8,128)S(1)} fusion(f32[4,196,16]{1,2,0:T(8,128)S(1)} %fusion.23, f32[4,196,16]{1,2,0:T(8,128)S(1)} %convolution_bitcast_fusion, bf16[4,196,768]{2,0,1:T(4,128)(2,1)} %param.6, f32[4,196,16]{1,2,0:T(8,128)S(1)} %copy-done.4, f32[4,16]{1,0:T(4,128)S(1)} %get-tuple-element.18), kind=kOutput, calls=%fused_computation.33 | convolution fusion | flops 19355652 | bytes 1404160 | tf_op jit(solution)/shard_map/bmd,bms->ds/dot_general | solution.py:85
  96.3 39.8 %psum.7 = f32[768,16]{0,1:T(8,128)} all-reduce(f32[768,16]{0,1:T(8,128)S(1)} %convolution_bitcast_fusion.1), channel_id=1, replica_groups=mesh['expert'=8,'pair'=2,'dp'=2] {'expert','pair','dp'}, use_global_device_ids=true, to_apply=%region_7.0 | all-reduce | flops 12288 | bytes 98304 | tf_op jit(solution)/shard_map/psum | solution.py:86
  136.1 3.9 %reshape_bitcast_fusion = bf16[1,1536,384]{1,0,2:T(2,128)(2,1)} fusion(bf16[384,1536]{1,0:T(8,128)(2,1)} %reduce-scatter.10.cloned.1.call-done), kind=kLoop, calls=%fused_computation.10 | loop fusion | bytes 2359296
  140.1 6.4 %copy.45 = bf16[1,1536,384]{2,1,0:T(8,128)(2,1)} copy(bf16[1,1536,384]{1,0,2:T(2,128)(2,1)} %reshape_bitcast_fusion) | data formatting | bytes 2359296
  (20 shorter events, 0.2 us)
Async XLA Ops:
  7.2 31.8 %copy-start = (bf16[1,768,1536]{2,1,0:T(8,128)(2,1)S(1)}, bf16[1,768,1536]{2,1,0:T(8,128)(2,1)}, u32[]{:S(2)}) copy-start(bf16[1,768,1536]{2,1,0:T(8,128)(2,1)} %param.8) | copy-start | bytes 7077892
  9.0 12.7 %copy-start.2 = (f32[4,196,16]{1,2,0:T(8,128)}, f32[4,196,16]{1,2,0:T(8,128)S(1)}, u32[]{:S(2)}) copy-start(f32[4,196,16]{1,2,0:T(8,128)S(1)} %fusion.32) | copy-start | bytes 150532
  12.1 14.4 %all-to-all-start = ((bf16[4,8,2,768]{3,2,0,1:T(2,128)(2,1)}), bf16[4,8,2,768]{3,2,0,1:T(2,128)(2,1)S(1)}, u32[]{:S(2)}, u32[]{:S(2)}) async-start(bf16[4,8,2,768]{3,2,0,1:T(2,128)(2,1)} %copy.32), calls=%async_computation | async-start | bytes 196608 | tf_op jit(solution)/shard_map/all_to_all | solution.py:49
  26.5 10.4 %all-to-all-start.1 = ((bf16[4,8,2,768]{3,2,0,1:T(2,128)(2,1)}), bf16[4,8,2,768]{3,2,0,1:T(2,128)(2,1)S(1)}, u32[]{:S(2)}, u32[]{:S(2)}) async-start(bf16[4,8,2,768]{3,2,0,1:T(2,128)(2,1)} %copy.35), calls=%async_computation.1 | async-start | bytes 196608 | tf_op jit(solution)/shard_map/all_to_all | solution.py:48
  29.8 42.0 %reduce-scatter.6.cloned.1.call-start = ((), (), s32[]{:S(2)}) async-start(), calls=%async_computation.6 | async-start | bytes 589824 | tf_op jit(solution)/shard_map/reduce_scatter | solution.py:62
  38.9 1.7 %copy-start.7 = (bf16[1,1536,768]{2,1,0:T(8,128)(2,1)S(1)}, bf16[1,1536,768]{2,1,0:T(8,128)(2,1)}, u32[]{:S(2)}) copy-start(bf16[1,1536,768]{2,1,0:T(8,128)(2,1)} %param.9) | copy-start | bytes 7077892
  46.9 89.2 %reduce-scatter.10.cloned.1.call-start = ((), (), s32[]{:S(2)}) async-start(), calls=%async_computation.8 | async-start | bytes 3538944
  65.8 1.0 copy-start.1
  65.9 80.6 %reduce-scatter.8.cloned.1.call-start = ((), (), s32[]{:S(2)}) async-start(), calls=%async_computation.7 | async-start | bytes 3538944 | tf_op jit(solution)/shard_map/reduce_scatter | solution.py:63
  69.1 0.9 copy-start.8
  70.0 7.1 %copy-start.5 = (f32[4,196,16]{1,2,0:T(8,128)S(1)}, f32[4,196,16]{1,2,0:T(8,128)}, u32[]{:S(2)}) copy-start(f32[4,196,16]{1,2,0:T(8,128)} %get-tuple-element.17) | copy-start | bytes 150532
  73.5 12.4 %copy-start.4 = (f32[4,196,16]{1,2,0:T(8,128)S(1)}, f32[4,196,16]{1,2,0:T(8,128)}, u32[]{:S(2)}) copy-start(f32[4,196,16]{1,2,0:T(8,128)} %get-tuple-element.19) | copy-start | bytes 150532
  73.5 12.4 %copy-start.6 = (bf16[768,16]{0,1:T(8,128)(2,1)S(1)}, bf16[768,16]{0,1:T(8,128)(2,1)}, u32[]{:S(2)}) copy-start(bf16[768,16]{0,1:T(8,128)(2,1)} %param.7) | copy-start | bytes 73732
  73.5 10.6 %all-to-all-start.2 = ((bf16[32,1,2,768]{3,2,1,0:T(2,128)(2,1)}), bf16[32,1,2,768]{3,2,1,0:T(2,128)(2,1)S(1)}, u32[]{:S(2)}, u32[]{:S(2)}) async-start(bf16[32,1,2,768]{3,2,1,0:T(2,128)(2,1)} %copy.38), calls=%async_computation.3 | async-start | bytes 196608 | tf_op jit(solution)/shard_map/all_to_all | solution.py:70
  85.9 2.2 %copy-start.3 = (f32[4,196,16]{1,2,0:T(8,128)S(1)}, f32[4,196,16]{1,2,0:T(8,128)}, u32[]{:S(2)}) copy-start(f32[4,196,16]{1,2,0:T(8,128)} %copy-done.2) | copy-start | bytes 150532
Sparse Core Ops, SparseCore 0:
  47.1 5.4 reduce-scatter.5
  66.0 32.4 reduce-scatter.9
  101.3 35.5 reduce-scatter.7
where the time goes:
time: 154 us; the launch traced here: 153 us
  blocking collectives  43.7 us (28%)
  local copies, waits for them, and re-layouts  37.2 us (24%)
  matrix products  25.5 us (17%)
  waiting for transfers between devices  15.9 us (10%)
  starting transfers between devices  14.3 us (9%)
  between operations  13.9 us (9%)
  other arithmetic  2.6 us (2%)
    psum x1, blocking collectives, local(): phi_grad = lax.psum(phi_part, ('expert', 'pair', 'dp'))  39.8 us
    unnamed x23, local copies, waits for them, and re-layouts  32.8 us
    all_to_all x1, starting transfers between devices, local(): lax.all_to_all(outgoing_grad, 'expert', split_axis=1, concat_axis=0, tile...  7.28 us
    all_to_all x1, waiting for transfers between devices, local(): lax.all_to_all(back_low, 'expert', split_axis=0, concat_axis=1, tiled=True)  6.84 us
    all_to_all x1, waiting for transfers between devices, local(): lax.all_to_all(outgoing_in, 'expert', split_axis=1, concat_axis=0, tiled=...  4.98 us
    all_to_all x1, waiting for transfers between devices, local(): lax.all_to_all(outgoing_grad, 'expert', split_axis=1, concat_axis=0, tile...  4.02 us
    dot_general x1, matrix products, local(): jnp.einsum('bms,bsd->bmd', dispatch_low, slot_in_grad, preferred_element_...  3.6 us
    all_to_all x1, starting transfers between devices, local(): lax.all_to_all(back_low, 'expert', split_axis=0, concat_axis=1, tiled=True)  3.49 us
  transfers between devices with their start and end apart: 6, of which 3 were waited for; matrix products, arithmetic and copies ran while one was open for 33% of the time, Pallas kernels for 0%

commit v1 on v0

v1 whole, which is shorter than its diff:
```python
import functools
import math

import jax
import jax.numpy as jnp
from jax import lax
from jax.experimental import pallas as pl
from jax.experimental.pallas import tpu as pltpu
from jax.sharding import PartitionSpec as P

MESH = pl.DeviceIdType.MESH
F32 = jnp.float32
BF16 = jnp.bfloat16
NN = (((1,), (0,)), ((), ()))
NT = (((1,), (1,)), ((), ()))
TN = (((0,), (0,)), ((), ()))


def mm(a, b, dims):
    return lax.dot_general(a, b, dims, preferred_element_type=F32)


def chunk_of(size):
    for width in (512, 384, 256, 128):
        if size % width == 0:
            return width
    return size


def kernel(
    n_e, n_p, n_d,
    tok_hbm, phi_ref, win_hbm, wout_hbm, so_hbm, go_hbm,
    tg_hbm, phit_ref, gw1_hbm, gw2_hbm,
    tok, go, so, win, wout, disp, comb, low, sp, stack, zg, recv, act, dpre,
    back, bin_, ret, sigr, phi_acc, ps, pr, qb, fin, tg, gw1, gw2,
    in_sem, w_sem, out_sem,
    a_send, a_recv, y_send, y_recv, c_send, c_recv, c2_send, c2_recv,
    b_send, b_recv, r_send, r_recv, p_send, p_recv, q_send, q_recv, f_send, f_recv, own_sem,
):
    e = lax.axis_index("expert")
    p = lax.axis_index("pair")
    d = lax.axis_index("dp")
    images, toks, width = tok.shape
    slots_all = phit_ref.shape[0]
    rows = zg.shape[2]
    slots = rows // images
    hidden = win.shape[1]
    fc = chunk_of(hidden)
    half = width // n_d

    def dev(ee, pp, dd):
        return {"expert": ee, "pair": pp, "dp": dd}

    def rem(x, n):
        return lax.rem(x, n)

    def rcopy(src, dst, ss, rs, where):
        return pltpu.make_async_remote_copy(
            src_ref=src, dst_ref=dst, send_sem=ss, recv_sem=rs, device_id=where, device_id_type=MESH
        )

    e_at = [rem(e + k, n_e) for k in range(n_e)]
    e_from = [rem(e + n_e - k, n_e) for k in range(n_e)]
    p_at = [rem(p + k, n_p) for k in range(n_p)]
    p_from = [rem(p + n_p - k, n_p) for k in range(n_p)]
    d_at = [rem(d + k, n_d) for k in range(n_d)]
    d_from = [rem(d + n_d - k, n_d) for k in range(n_d)]

    barrier = pltpu.get_barrier_semaphore()
    peers = [dev(e_at[k], p, d) for k in range(1, n_e)]
    peers += [dev(e, p_at[i], d_at[j]) for i in range(n_p) for j in range(n_d) if i or j]
    for peer in peers:
        pl.semaphore_signal(barrier, inc=1, device_id=peer, device_id_type=MESH)

    loads = []
    for b in range(images):
        pair = (
            pltpu.make_async_copy(tok_hbm.at[b], tok.at[b], in_sem.at[2 * b]),
            pltpu.make_async_copy(go_hbm.at[b], go.at[b], in_sem.at[2 * b + 1]),
        )
        pair[0].start()
        pair[1].start()
        loads.append(pair)
    w_loads = [
        pltpu.make_async_copy(win_hbm.at[0], win, w_sem.at[0]),
        pltpu.make_async_copy(wout_hbm.at[0], wout, w_sem.at[1]),
        pltpu.make_async_copy(so_hbm, so, w_sem.at[2]),
    ]
    for w_load in w_loads:
        w_load.start()

    phi_t = phi_ref[...].astype(F32).T.astype(BF16)
    total = images * slots_all
    r_at = lax.broadcasted_iota(jnp.int32, (total, total), 0)
    c_at = lax.broadcasted_iota(jnp.int32, (total, total), 1)
    src_of = ((r_at % rows) // slots) * slots_all + (r_at // rows) * slots + r_at % slots
    perm = jnp.where(src_of == c_at, 1.0, 0.0).astype(BF16)

    for b in range(images):
        loads[b][0].wait()
        logits = mm(phi_t, tok[b], NT)
        by_tok = jnp.exp(logits - jnp.max(logits, axis=1, keepdims=True))
        by_tok = by_tok / jnp.sum(by_tok, axis=1, keepdims=True)
        by_slot = jnp.exp(logits - jnp.max(logits, axis=0, keepdims=True))
        by_slot = by_slot / jnp.sum(by_slot, axis=0, keepdims=True)
        disp[b] = by_tok
        comb[b] = by_slot
        low[b, pl.ds(0, slots_all), :] = by_tok.astype(BF16)
        stack[0, pl.ds(b * slots_all, slots_all), :] = mm(by_tok.astype(BF16), tok[b], NN).astype(BF16)
        loads[b][1].wait()
        stack[1, pl.ds(b * slots_all, slots_all), :] = mm(by_slot.astype(BF16), go[b], NN).astype(BF16)
    for which in range(2):
        moved = mm(perm, stack[which], NN).astype(BF16)
        zg[which] = moved.reshape(n_e, rows, width)

    pl.semaphore_wait(barrier, len(peers))

    out_a = []
    for k in range(1, n_e):
        cp = rcopy(
            zg.at[:, e_at[k]], recv.at[:, d, p, e], a_send.at[k], a_recv.at[k], dev(e_at[k], p, d)
        )
        cp.start()
        out_a.append(cp)
    own = pltpu.make_async_copy(zg.at[:, e], recv.at[:, d, p, e], own_sem.at[0])
    own.start()

    w_loads[2].wait()
    for b in range(images):
        cg = mm(so[b], go[b], NT)
        cm = comb[b]
        comb[b] = cm * (cg - jnp.sum(cm * cg, axis=0, keepdims=True))

    out_y, out_c, out_c2 = [], [], []
    for k in range(n_e):
        blk = recv.at[:, d, p, e_from[k]]
        if k == 0:
            own.wait()
        else:
            rcopy(blk, blk, a_send.at[k], a_recv.at[k], dev(e, p, d)).wait_recv()
        for i in range(1, n_p):
            cp = rcopy(blk, blk, c_send.at[i, k], c_recv.at[i, k], dev(e, p_at[i], d))
            cp.start()
            out_c.append(cp)
        for j in range(1, n_d):
            cp = rcopy(blk, blk, y_send.at[j, k], y_recv.at[j, k], dev(e, p, d_at[j]))
            cp.start()
            out_y.append(cp)
    for cp in w_loads[:2]:
        cp.wait()
    for i in range(1, n_p):
        for k in range(n_e):
            blk = recv.at[:, d, p_from[i], e_from[k]]
            rcopy(blk, blk, c_send.at[i, k], c_recv.at[i, k], dev(e, p, d)).wait_recv()

    group_rows = n_p * n_e * rows
    part_rows = n_e * rows
    c1 = math.sqrt(2.0 / math.pi)

    def hidden_pass(group, with_back):
        z = recv[0, group].reshape(group_rows, width)
        g = recv[1, group].reshape(group_rows, width)

        def step(c, carry):
            cols = pl.ds(pl.multiple_of(c * fc, fc), fc)
            x = mm(z, win[:, cols], NN)
            da = mm(g, wout[cols, :], NT)
            x2 = x * x
            th = jnp.tanh(c1 * (x + 0.044715 * (x2 * x)))
            cdf = 0.5 * (1.0 + th)
            slope = cdf + (0.5 * c1) * x * (1.0 - th * th) * (1.0 + (3.0 * 0.044715) * x2)
            act[group, :, cols] = (x * cdf).astype(BF16)
            dp_low = (da * slope).astype(BF16)
            dpre[group, :, cols] = dp_low
            if with_back:
                term = mm(dp_low, win[:, cols], NT).reshape(n_p, part_rows, width)

                @pl.when(c == 0)
                def _():
                    back[...] = term

                @pl.when(c > 0)
                def _():
                    back[...] = back[...] + term

            return carry

        lax.fori_loop(0, hidden // fc, step, 0)

    hidden_pass(d, True)

    out_b = []
    for i in range(1, n_p):
        cp = rcopy(back.at[p_at[i]], bin_.at[i - 1], b_send.at[i], b_recv.at[i], dev(e, p_at[i], d))
        cp.start()
        out_b.append(cp)

    for j in range(1, n_d):
        for k in range(n_e):
            blk = recv.at[:, d_from[j], p, e_from[k]]
            rcopy(blk, blk, y_send.at[j, k], y_recv.at[j, k], dev(e, p, d)).wait_recv()
            for i in range(1, n_p):
                cp = rcopy(blk, blk, c2_send.at[j, i, k], c2_recv.at[j, i, k], dev(e, p_at[i], d))
                cp.start()
                out_c2.append(cp)

    acc = back[p]
    for i in range(1, n_p):
        rcopy(bin_.at[i - 1], bin_.at[i - 1], b_send.at[i], b_recv.at[i], dev(e, p, d)).wait_recv()
        acc = acc + bin_[i - 1]
    ret[...] = acc.astype(BF16).reshape(n_e, rows, width)
    out_r = []
    for k in range(1, n_e):
        cp = rcopy(ret.at[e_at[k]], sigr.at[e], r_send.at[k], r_recv.at[k], dev(e_at[k], p, d))
        cp.start()
        out_r.append(cp)
    sigr[e] = ret[e]

    for j in range(1, n_d):
        for i in range(1, n_p):
            for k in range(n_e):
                blk = recv.at[:, d_from[j], p_from[i], e_from[k]]
                rcopy(blk, blk, c2_send.at[j, i, k], c2_recv.at[j, i, k], dev(e, p, d)).wait_recv()
        hidden_pass(d_from[j], False)

    my_half = pl.ds(pl.multiple_of(d * half, half), half)

    def grads_in(c, carry):
        cols = pl.ds(pl.multiple_of(c * fc, fc), fc)
        s1 = None
        for gi in range(n_d):
            z = recv[0, gi, :, :, :, my_half].reshape(group_rows, half)
            g1 = mm(z, dpre[gi, :, cols], TN).astype(BF16).astype(F32)
            s1 = g1 if s1 is None else s1 + g1
        gw1[:, cols] = s1.astype(BF16)
        return carry

    def grads_out(c, carry):
        cols = pl.ds(pl.multiple_of(c * fc, fc), fc)
        s2 = None
        for gi in range(n_d):
            g = recv[1, gi, :, :, :, my_half].reshape(group_rows, half)
            g2 = mm(act[gi, :, cols], g, TN).astype(BF16).astype(F32)
            s2 = g2 if s2 is None else s2 + g2
        gw2[cols, :] = s2.astype(BF16)
        return carry

    lax.fori_loop(0, hidden // fc, grads_in, 0)
    outs = [pltpu.make_async_copy(gw1, gw1_hbm.at[0], out_sem.at[0])]
    outs[0].start()

    for k in range(1, n_e):
        blk = sigr.at[e_from[k]]
        rcopy(blk, blk, r_send.at[k], r_recv.at[k], dev(e, p, d)).wait_recv()

    sig_all = mm(perm, sigr[...].reshape(total, width), TN).astype(BF16)
    phi_sum = None
    for b in range(images):
        sig = sig_all[b * slots_all:(b + 1) * slots_all]
        sp[b, pl.ds(0, slots_all), :] = sig
        sp[b, pl.ds(slots_all, slots_all), :] = phi_t
        dg = mm(sig, tok[b], NT)
        dm = disp[b]
        lg = dm * (dg - jnp.sum(dm * dg, axis=1, keepdims=True)) + comb[b]
        lg_low = lg.astype(BF16)
        low[b, pl.ds(slots_all, slots_all), :] = lg_low
        term = mm(lg_low, tok[b], NN)
        phi_sum = term if phi_sum is None else phi_sum + term
    phi_acc[...] = phi_sum
    for k in range(n_e):
        ps[k] = phi_acc[pl.ds(k * slots, slots), :]
    out_p = []
    for k in range(1, n_e):
        cp = rcopy(ps.at[e_at[k]], pr.at[e], p_send.at[k], p_recv.at[k], dev(e_at[k], p, d))
        cp.start()
        out_p.append(cp)
    pr[e] = ps[e]

    for b in range(images):
        tg[b] = mm(low[b], sp[b], TN).astype(BF16)
        cp = pltpu.make_async_copy(tg.at[b], tg_hbm.at[b], out_sem.at[2 + b])
        cp.start()
        outs.append(cp)

    for k in range(1, n_e):
        blk = pr.at[e_from[k]]
        rcopy(blk, blk, p_send.at[k], p_recv.at[k], dev(e, p, d)).wait_recv()
    qb[d, p] = jnp.sum(pr[...], axis=0)
    out_q = []
    for j in range(n_d):
        for i in range(n_p):
            if i or j:
                cp = rcopy(
                    qb.at[d, p], qb.at[d, p], q_send.at[j, i], q_recv.at[j, i], dev(e, p_at[i], d_at[j])
                )
                cp.start()
                out_q.append(cp)

    lax.fori_loop(0, hidden // fc, grads_out, 0)
    cp = pltpu.make_async_copy(gw2, gw2_hbm.at[0], out_sem.at[1])
    cp.start()
    outs.append(cp)

    for j in range(n_d):
        for i in range(n_p):
            if i or j:
                blk = qb.at[d_from[j], p_from[i]]
                rcopy(blk, blk, q_send.at[j, i], q_recv.at[j, i], dev(e, p, d)).wait_recv()
    whole = None
    for j in range(n_d):
        for i in range(n_p):
            whole = qb[j, i] if whole is None else whole + qb[j, i]
    fin[e] = whole
    out_f = []
    for k in range(1, n_e):
        cp = rcopy(fin.at[e], fin.at[e], f_send.at[k], f_recv.at[k], dev(e_at[k], p, d))
        cp.start()
        out_f.append(cp)
    for group in (out_a, out_y, out_c, out_c2, out_b, out_r, out_p, out_q):
        for cp in group:
            cp.wait_send()
    for cp in outs:
        cp.wait()
    for k in range(1, n_e):
        blk = fin.at[e_from[k]]
        rcopy(blk, blk, f_send.at[k], f_recv.at[k], dev(e, p, d)).wait_recv()
    for k in range(n_e):
        phit_ref[pl.ds(k * slots, slots), :] = fin[k]
    for cp in out_f:
        cp.wait_send()


def local(n_e, n_p, n_d, tokens, phi, w_in, w_out, slot_out, grad_out):
    images, toks, width = tokens.shape
    slots_all = phi.shape[1]
    hidden = w_in.shape[2]
    slots = slots_all // n_e
    rows = images * slots
    half = width // n_d
    group = n_p * n_e * rows
    vm = pltpu.VMEM
    sem = pltpu.SemaphoreType.DMA
    scratch = [
        vm((images, toks, width), BF16),
        vm((images, toks, width), BF16),
        vm((images, slots_all, width), BF16),
        vm((width, hidden), BF16),
        vm((hidden, width), BF16),
        vm((images, slots_all, toks), F32),
        vm((images, slots_all, toks), F32),
        vm((images, 2 * slots_all, toks), BF16),
        vm((images, 2 * slots_all, width), BF16),
        vm((2, images * slots_all, width), BF16),
        vm((2, n_e, rows, width), BF16),
        vm((2, n_d, n_p, n_e, rows, width), BF16),
        vm((n_d, group, hidden), BF16),
        vm((n_d, group, hidden), BF16),
        vm((n_p, n_e * rows, width), F32),
        vm((n_p - 1, n_e * rows, width), F32),
        vm((n_e, rows, width), BF16),
        vm((n_e, rows, width), BF16),
        vm((slots_all, width), F32),
        vm((n_e, slots, width), F32),
        vm((n_e, slots, width), F32),
        vm((n_d, n_p, slots, width), F32),
        vm((n_e, slots, width), F32),
        vm((images, toks, width), BF16),
        vm((half, hidden), BF16),
        vm((hidden, half), BF16),
        sem((2 * images,)),
        sem((3,)),
        sem((2 + images,)),
    ]
    scratch += [sem((n_e,))] * 2
    scratch += [sem((n_d, n_e))] * 2
    scratch += [sem((n_p, n_e))] * 2
    scratch += [sem((n_d, n_p, n_e))] * 2
    scratch += [sem((n_p,))] * 2
    scratch += [sem((n_e,))] * 2
    scratch += [sem((n_e,))] * 2
    scratch += [sem((n_d, n_p))] * 2
    scratch += [sem((n_e,))] * 2
    scratch += [sem((1,))]
    hbm = pl.BlockSpec(memory_space=pl.ANY)
    vmem = pl.BlockSpec(memory_space=pltpu.VMEM)
    token_grad, phi_t, gw1, gw2 = pl.pallas_call(
        functools.partial(kernel, n_e, n_p, n_d),
        out_shape=(
            jax.ShapeDtypeStruct((images, toks, width), BF16),
            jax.ShapeDtypeStruct((slots_all, width), F32),
            jax.ShapeDtypeStruct((1, half, hidden), BF16),
            jax.ShapeDtypeStruct((1, hidden, half), BF16),
        ),
        in_specs=[hbm, vmem, hbm, hbm, hbm, hbm],
        out_specs=(hbm, vmem, hbm, hbm),
        scratch_shapes=scratch,
        compiler_params=pltpu.CompilerParams(collective_id=0, has_side_effects=True),
    )(tokens, phi, w_in, w_out, slot_out, grad_out)
    return (token_grad, phi_t.T, gw1, gw2)


def solution(mesh):
    in_specs = (
        P(("expert", "pair", "dp"), None, None),
        P(),
        P("expert", None, "pair"),
        P("expert", "pair", None),
        P(("expert", "pair", "dp"), None, None),
        P(("expert", "pair", "dp"), None, None),
    )
    out_specs = (
        P(("expert", "pair", "dp"), None, None),
        P(),
        P("expert", "dp", "pair"),
        P("expert", "pair", "dp"),
    )
    body = functools.partial(local, mesh.shape["expert"], mesh.shape["pair"], mesh.shape["dp"])
    return jax.shard_map(body, mesh=mesh, in_specs=in_specs, out_specs=out_specs, check_vma=False)
```

time: 154 us -> 51 us (0.33)
  blocking collectives: 43.7 us -> 0 us
  Pallas kernels: 0 us -> 38.6 us
  local copies, waits for them, and re-layouts: 37.2 us -> 11.5 us
  matrix products: 25.5 us -> 0 us
  waiting for transfers between devices: 15.9 us -> 0 us
  starting transfers between devices: 14.3 us -> 0 us
  between operations: 13.9 us -> 0.66 us
  other arithmetic: 2.6 us -> 0 us
    psum x1 -> x0, blocking collectives: 39.8 us -> none  [local(): phi_grad = lax.psum(phi_part, ('expert', 'pair', 'dp'))]
    pallas_call x0 -> x1, Pallas kernels: none -> 38.6 us  [local(): pl.pallas_call(functools.partial(kernel, n_e, n_p, n_d), out_shape=(jax.S...]
    dot_general x13 -> x0, matrix products: 25.5 us -> none  [the longest x1 3.6 us: local(): jnp.einsum('bms,bsd->bmd', dispatch_low, slot_in_grad, preferred_element_...]
    unnamed x23 -> x15, local copies, waits for them, and re-layouts: 32.8 us -> 11.5 us
    all_to_all x3 -> x0, waiting for transfers between devices: 15.8 us -> none  [the longest x1 6.84 us: local(): lax.all_to_all(back_low, 'expert', split_axis=0, concat_axis=1, tiled=True)]
    all_to_all x3 -> x0, starting transfers between devices: 14.1 us -> none  [the longest x1 7.28 us: local(): lax.all_to_all(outgoing_grad, 'expert', split_axis=1, concat_axis=0, tile...]
    all_gather x2 -> x0, blocking collectives: 3.88 us -> none  [the longest x1 1.95 us: local(): lax.all_gather(arrived_grad, 'pair', axis=0, tiled=True)]
    another operation x3 -> x0, local copies, waits for them, and re-layouts: 2.04 us -> none
  transfers between devices with their start and end apart: 6 -> 0, of which waited for: 3 -> 0; matrix products, arithmetic and copies ran while one was open for 33% -> 0% of each run, Pallas kernels for 0% -> 0%
where the time goes in v1:
time: 51 us; the launch traced here: 50.7 us
  Pallas kernels  38.6 us (76%)
  local copies, waits for them, and re-layouts  11.5 us (23%)
  between operations  0.66 us (1%)
    pallas_call x1, Pallas kernels, local(): pl.pallas_call(functools.partial(kernel, n_e, n_p, n_d), out_shape=(jax.S...  38.6 us
    unnamed x15, local copies, waits for them, and re-layouts  11.5 us

profile of v1, /device:TPU:0, one launch (start us, length us, event | category | flops | bytes accessed | tf_op | source)
XLA Modules:
  0.0 50.7 jit_solution(11427460333347528992)
XLA Ops:
  0.6 1.6 %copy.11.phi_ref = bf16[768,16]{1,0:T(8,128)(2,1)} copy(bf16[768,16]{0,1:T(8,128)(2,1)} %param.7) | data formatting | bytes 49152 | tf_op args[1]
  2.2 0.0 copy-start
  2.2 2.5 %copy.10.tok_hbm = bf16[4,196,768]{2,1,0:T(8,128)(2,1)} copy(bf16[4,196,768]{2,0,1:T(4,128)(2,1)} %param.6) | data formatting | bytes 2408448 | tf_op args[0]
  4.7 0.0 copy-done
  4.7 1.2 %copy.12.go_hbm = bf16[4,196,768]{2,1,0:T(8,128)(2,1)} copy(bf16[4,196,768]{2,0,1:T(4,128)(2,1)S(1)} %copy-done) | data formatting | bytes 2408448 | tf_op args[5]
  5.9 38.6 %shard_map.93 = (bf16[4,196,768]{2,1,0:T(8,128)(2,1)}, f32[16,768]{1,0:T(8,128)}, bf16[1,384,1536]{2,1,0:T(8,128)(2,1)}, bf16[1,1536,384]{2,1,0:T(8,128)(2,1)}) custom-call(bf16[4,196,768]{2,1,0:T(8,128)(2,1)} %copy.10.tok_hbm, bf16[768,16]{1,0:T(8,128)(2,1)} %copy.11.phi_ref, bf16[1,768,1536]{2,1,0:T(8,128)(2,1)} %win_hbm.1, ...), custom_call_target="tpu_custom_call" | custom-call | tf_op jit(solution)/shard_map/pallas_call | solution.py:386
  44.5 0.0 copy-start.3
  44.5 0.0 copy-start.2
  44.5 2.9 %copy.13 = bf16[4,196,768]{2,0,1:T(4,128)(2,1)} copy(bf16[4,196,768]{2,1,0:T(8,128)(2,1)} %get-tuple-element.12) | data formatting | bytes 2408448
  47.4 0.0 copy-done.3
  47.4 0.6 %copy.17 = f32[768,16]{0,1:T(8,128)} copy(f32[768,16]{0,1:T(8,128)S(1)} %bitcast.1) | data formatting | bytes 98304
  48.0 0.0 copy-done.2
  48.0 0.0 copy-start.1
  48.0 1.0 %copy.18 = bf16[1,384,1536]{2,1,0:T(8,128)(2,1)} copy(bf16[1,384,1536]{2,1,0:T(8,128)(2,1)S(1)} %copy-done.2) | data formatting | bytes 2359296
  49.0 0.7 %copy-done.1 = bf16[1,1536,384]{2,1,0:T(8,128)(2,1)S(1)} copy-done((bf16[1,1536,384]{2,1,0:T(8,128)(2,1)S(1)}, bf16[1,1536,384]{2,1,0:T(8,128)(2,1)}, u32[]{:S(2)}) %copy-start.1) | copy-done | bytes 1179672
  49.7 1.0 %copy.19 = bf16[1,1536,384]{2,1,0:T(8,128)(2,1)} copy(bf16[1,1536,384]{2,1,0:T(8,128)(2,1)S(1)} %copy-done.1) | data formatting | bytes 2359296
Async XLA Ops:
  2.2 2.5 %copy-start = (bf16[4,196,768]{2,0,1:T(4,128)(2,1)S(1)}, bf16[4,196,768]{2,0,1:T(4,128)(2,1)}, u32[]{:S(2)}) copy-start(bf16[4,196,768]{2,0,1:T(4,128)(2,1)} %param.11) | copy-start | bytes 3612676
  44.5 2.9 %copy-start.3 = (f32[16,768]{1,0:T(8,128)S(1)}, f32[16,768]{1,0:T(8,128)}, u32[]{:S(2)}) copy-start(f32[16,768]{1,0:T(8,128)} %get-tuple-element.9) | copy-start | bytes 147460
  44.5 3.5 %copy-start.2 = (bf16[1,384,1536]{2,1,0:T(8,128)(2,1)S(1)}, bf16[1,384,1536]{2,1,0:T(8,128)(2,1)}, u32[]{:S(2)}) copy-start(bf16[1,384,1536]{2,1,0:T(8,128)(2,1)} %get-tuple-element.22) | copy-start | bytes 3538948
  48.0 1.7 %copy-start.1 = (bf16[1,1536,384]{2,1,0:T(8,128)(2,1)S(1)}, bf16[1,1536,384]{2,1,0:T(8,128)(2,1)}, u32[]{:S(2)}) copy-start(bf16[1,1536,384]{2,1,0:T(8,128)(2,1)} %get-tuple-element.23) | copy-start | bytes 3538948

commit v2 on v1

--- a/solution.py
+++ b/solution.py
@@ -31,7 +31,7 @@
     n_e, n_p, n_d,
     tok_hbm, phi_ref, win_hbm, wout_hbm, so_hbm, go_hbm,
     tg_hbm, phit_ref, gw1_hbm, gw2_hbm,
-    tok, go, so, win, wout, disp, comb, low, sp, stack, zg, recv, act, dpre,
+    tok3, go3, tok, go, so, win, wout, disp, comb, low, sp, zg, recv, act, dpre,
     back, bin_, ret, sigr, phi_acc, ps, pr, qb, fin, tg, gw1, gw2,
     in_sem, w_sem, out_sem,
     a_send, a_recv, y_send, y_recv, c_send, c_recv, c2_send, c2_recv,
@@ -40,7 +40,7 @@
     e = lax.axis_index("expert")
     p = lax.axis_index("pair")
     d = lax.axis_index("dp")
-    images, toks, width = tok.shape
+    toks, images, width = tok3.shape
     slots_all = phit_ref.shape[0]
     rows = zg.shape[2]
     slots = rows // images
@@ -72,15 +72,12 @@
     for peer in peers:
         pl.semaphore_signal(barrier, inc=1, device_id=peer, device_id_type=MESH)
 
-    loads = []
-    for b in range(images):
-        pair = (
-            pltpu.make_async_copy(tok_hbm.at[b], tok.at[b], in_sem.at[2 * b]),
-            pltpu.make_async_copy(go_hbm.at[b], go.at[b], in_sem.at[2 * b + 1]),
-        )
-        pair[0].start()
-        pair[1].start()
-        loads.append(pair)
+    loads = [
+        pltpu.make_async_copy(tok_hbm, tok3, in_sem.at[0]),
+        pltpu.make_async_copy(go_hbm, go3, in_sem.at[1]),
+    ]
+    for load in loads:
+        load.start()
     w_loads = [
         pltpu.make_async_copy(win_hbm.at[0], win, w_sem.at[0]),
         pltpu.make_async_copy(wout_hbm.at[0], wout, w_sem.at[1]),
@@ -89,29 +86,40 @@
     for w_load in w_loads:
         w_load.start()
 
-    phi_t = phi_ref[...].astype(F32).T.astype(BF16)
     total = images * slots_all
-    r_at = lax.broadcasted_iota(jnp.int32, (total, total), 0)
-    c_at = lax.broadcasted_iota(jnp.int32, (total, total), 1)
-    src_of = ((r_at % rows) // slots) * slots_all + (r_at // rows) * slots + r_at % slots
-    perm = jnp.where(src_of == c_at, 1.0, 0.0).astype(BF16)
-
-    for b in range(images):
-        loads[b][0].wait()
-        logits = mm(phi_t, tok[b], NT)
-        by_tok = jnp.exp(logits - jnp.max(logits, axis=1, keepdims=True))
-        by_tok = by_tok / jnp.sum(by_tok, axis=1, keepdims=True)
-        by_slot = jnp.exp(logits - jnp.max(logits, axis=0, keepdims=True))
-        by_slot = by_slot / jnp.sum(by_slot, axis=0, keepdims=True)
-        disp[b] = by_tok
-        comb[b] = by_slot
-        low[b, pl.ds(0, slots_all), :] = by_tok.astype(BF16)
-        stack[0, pl.ds(b * slots_all, slots_all), :] = mm(by_tok.astype(BF16), tok[b], NN).astype(BF16)
-        loads[b][1].wait()
-        stack[1, pl.ds(b * slots_all, slots_all), :] = mm(by_slot.astype(BF16), go[b], NN).astype(BF16)
-    for which in range(2):
-        moved = mm(perm, stack[which], NN).astype(BF16)
-        zg[which] = moved.reshape(n_e, rows, width)
+    lanes = toks * images
+
+    def pick(columns, index_of):
+        r_at = lax.broadcasted_iota(jnp.int32, (total, columns), 0)
+        c_at = lax.broadcasted_iota(jnp.int32, (total, columns), 1)
+        return jnp.where(index_of(r_at) == c_at, 1.0, 0.0).astype(BF16)
+
+    def slot_of(r):
+        return (r // rows) * slots + r % slots
+
+    def image_of(r):
+        return (r % rows) // slots
+
+    phi_x = mm(pick(slots_all, slot_of), phi_ref[...], NN).astype(BF16)
+    sp[pl.ds(total, total), :] = phi_x
+    r_at = lax.broadcasted_iota(jnp.int32, (total, lanes), 0)
+    l_at = lax.broadcasted_iota(jnp.int32, (total, lanes), 1)
+    same = image_of(r_at) == l_at % images
+
+    loads[0].wait()
+    tok[...] = tok3[...].reshape(lanes, width)
+    logits = jnp.where(same, mm(phi_x, tok[...], NT), -jnp.inf)
+    by_tok = jnp.exp(logits - jnp.max(logits, axis=1, keepdims=True))
+    by_tok = by_tok / jnp.sum(by_tok, axis=1, keepdims=True)
+    disp[...] = by_tok
+    low[pl.ds(0, total), :] = by_tok.astype(BF16)
+    zg[0] = mm(by_tok.astype(BF16), tok[...], NN).astype(BF16).reshape(n_e, rows, width)
+    by_slot = jnp.exp(logits - jnp.max(logits, axis=0, keepdims=True))
+    by_slot = by_slot / jnp.sum(by_slot, axis=0, keepdims=True)
+    comb[...] = by_slot
+    loads[1].wait()
+    go[...] = go3[...].reshape(lanes, width)
+    zg[1] = mm(by_slot.astype(BF16), go[...], NN).astype(BF16).reshape(n_e, rows, width)
 
     pl.semaphore_wait(barrier, len(peers))
 
@@ -126,10 +134,12 @@
     own.start()
 
     w_loads[2].wait()
-    for b in range(images):
-        cg = mm(so[b], go[b], NT)
-        cm = comb[b]
-        comb[b] = cm * (cg - jnp.sum(cm * cg, axis=0, keepdims=True))
+    so_x = mm(
+        pick(total, lambda r: image_of(r) * slots_all + slot_of(r)), so[...].reshape(total, width), NN
+    ).astype(BF16)
+    cm = comb[...]
+    cg = mm(so_x, go[...], NT)
+    comb[...] = cm * (cg - jnp.sum(cm * cg, axis=0, keepdims=True))
 
     out_y, out_c, out_c2 = [], [], []
     for k in range(n_e):
@@ -253,22 +263,17 @@
         blk = sigr.at[e_from[k]]
         rcopy(blk, blk, r_send.at[k], r_recv.at[k], dev(e, p, d)).wait_recv()
 
-    sig_all = mm(perm, sigr[...].reshape(total, width), TN).astype(BF16)
-    phi_sum = None
-    for b in range(images):
-        sig = sig_all[b * slots_all:(b + 1) * slots_all]
-        sp[b, pl.ds(0, slots_all), :] = sig
-        sp[b, pl.ds(slots_all, slots_all), :] = phi_t
-        dg = mm(sig, tok[b], NT)
-        dm = disp[b]
-        lg = dm * (dg - jnp.sum(dm * dg, axis=1, keepdims=True)) + comb[b]
-        lg_low = lg.astype(BF16)
-        low[b, pl.ds(slots_all, slots_all), :] = lg_low
-        term = mm(lg_low, tok[b], NN)
-        phi_sum = term if phi_sum is None else phi_sum + term
-    phi_acc[...] = phi_sum
+    sig = sigr[...].reshape(total, width)
+    dg = mm(sig, tok[...], NT)
+    dm = disp[...]
+    lg_low = (dm * (dg - jnp.sum(dm * dg, axis=1, keepdims=True)) + comb[...]).astype(BF16)
+    phi_acc[...] = mm(lg_low, tok[...], NN)
     for k in range(n_e):
-        ps[k] = phi_acc[pl.ds(k * slots, slots), :]
+        piece = None
+        for b in range(images):
+            term = phi_acc[pl.ds(k * rows + b * slots, slots), :]
+            piece = term if piece is None else piece + term
+        ps[k] = piece
     out_p = []
     for k in range(1, n_e):
         cp = rcopy(ps.at[e_at[k]], pr.at[e], p_send.at[k], p_recv.at[k], dev(e_at[k], p, d))
@@ -276,11 +281,12 @@
         out_p.append(cp)
     pr[e] = ps[e]
 
-    for b in range(images):
-        tg[b] = mm(low[b], sp[b], TN).astype(BF16)
-        cp = pltpu.make_async_copy(tg.at[b], tg_hbm.at[b], out_sem.at[2 + b])
-        cp.start()
-        outs.append(cp)
+    low[pl.ds(total, total), :] = lg_low
+    sp[pl.ds(0, total), :] = sig
+    tg[...] = mm(low[...], sp[...], TN).astype(BF16).reshape(toks, images, width)
+    cp = pltpu.make_async_copy(tg, tg_hbm, out_sem.at[2])
+    cp.start()
+    outs.append(cp)
 
     for k in range(1, n_e):
         blk = pr.at[e_from[k]]
@@ -341,16 +347,17 @@
     vm = pltpu.VMEM
     sem = pltpu.SemaphoreType.DMA
     scratch = [
-        vm((images, toks, width), BF16),
-        vm((images, toks, width), BF16),
+        vm((toks, images, width), BF16),
+        vm((toks, images, width), BF16),
+        vm((toks * images, width), BF16),
+        vm((toks * images, width), BF16),
         vm((images, slots_all, width), BF16),
         vm((width, hidden), BF16),
         vm((hidden, width), BF16),
-        vm((images, slots_all, toks), F32),
-        vm((images, slots_all, toks), F32),
-        vm((images, 2 * slots_all, toks), BF16),
-        vm((images, 2 * slots_all, width), BF16),
-        vm((2, images * slots_all, width), BF16),
+        vm((images * slots_all, toks * images), F32),
+        vm((images * slots_all, toks * images), F32),
+        vm((2 * images * slots_all, toks * images), BF16),
+        vm((2 * images * slots_all, width), BF16),
         vm((2, n_e, rows, width), BF16),
         vm((2, n_d, n_p, n_e, rows, width), BF16),
         vm((n_d, group, hidden), BF16),
@@ -359,17 +366,17 @@
         vm((n_p - 1, n_e * rows, width), F32),
         vm((n_e, rows, width), BF16),
         vm((n_e, rows, width), BF16),
-        vm((slots_all, width), F32),
+        vm((images * slots_all, width), F32),
         vm((n_e, slots, width), F32),
         vm((n_e, slots, width), F32),
         vm((n_d, n_p, slots, width), F32),
         vm((n_e, slots, width), F32),
-        vm((images, toks, width), BF16),
+        vm((toks, images, width), BF16),
         vm((half, hidden), BF16),
         vm((hidden, half), BF16),
-        sem((2 * images,)),
+        sem((2,)),
         sem((3,)),
-        sem((2 + images,)),
+        sem((3,)),
     ]
     scratch += [sem((n_e,))] * 2
     scratch += [sem((n_d, n_e))] * 2
@@ -386,7 +393,7 @@
     token_grad, phi_t, gw1, gw2 = pl.pallas_call(
         functools.partial(kernel, n_e, n_p, n_d),
         out_shape=(
-            jax.ShapeDtypeStruct((images, toks, width), BF16),
+            jax.ShapeDtypeStruct((toks, images, width), BF16),
             jax.ShapeDtypeStruct((slots_all, width), F32),
             jax.ShapeDtypeStruct((1, half, hidden), BF16),
             jax.ShapeDtypeStruct((1, hidden, half), BF16),
@@ -395,8 +402,10 @@
         out_specs=(hbm, vmem, hbm, hbm),
         scratch_shapes=scratch,
         compiler_params=pltpu.CompilerParams(collective_id=0, has_side_effects=True),
-    )(tokens, phi, w_in, w_out, slot_out, grad_out)
-    return (token_grad, phi_t.T, gw1, gw2)
+    )(
+        jnp.transpose(tokens, (1, 0, 2)), phi.T, w_in, w_out, slot_out, jnp.transpose(grad_out, (1, 0, 2))
+    )
+    return (jnp.transpose(token_grad, (1, 0, 2)), phi_t.T, gw1, gw2)
 
 
 def solution(mesh):

time: 51 us -> 43.4 us (0.85)
  local copies, waits for them, and re-layouts: 11.5 us -> 5.47 us
  Pallas kernels: 38.6 us -> 37.1 us
    unnamed x15 -> x10, local copies, waits for them, and re-layouts: 11.5 us -> 5.47 us
    pallas_call x1, Pallas kernels: 38.6 us -> 37.1 us  [local(): pl.pallas_call(functools.partial(kernel, n_e, n_p, n_d), out_shape=(jax.S...]
where the time goes in v2:
time: 43.4 us; the launch traced here: 43.2 us
  Pallas kernels  37.1 us (85%)
  local copies, waits for them, and re-layouts  5.47 us (13%)
  between operations  0.66 us (2%)
    pallas_call x1, Pallas kernels, local(): pl.pallas_call(functools.partial(kernel, n_e, n_p, n_d), out_shape=(jax.S...  37.1 us
    unnamed x10, local copies, waits for them, and re-layouts  5.47 us

profile of v2, /device:TPU:0, one launch (start us, length us, event | category | flops | bytes accessed | tf_op | source)
XLA Modules:
  0.0 43.2 jit_solution(11831088018207958687)
XLA Ops:
  0.6 37.1 %shard_map.93 = (bf16[196,4,768]{2,1,0:T(4,128)(2,1)}, f32[16,768]{1,0:T(8,128)}, bf16[1,384,1536]{2,1,0:T(8,128)(2,1)}, bf16[1,1536,384]{2,1,0:T(8,128)(2,1)}) custom-call(bf16[196,4,768]{2,1,0:T(4,128)(2,1)} %bitcast.6, bf16[16,768]{1,0:T(8,128)(2,1)} %bitcast.9, bf16[1,768,1536]{2,1,0:T(8,128)(2,1)} %win_hbm.1, bf16[1,1536,768]{2,1,0:T(8,128)(2,1)} %wout_hbm.1, ...), custom_call_target="tpu_custom_call" | custom-call | tf_op jit(solution)/shard_map/pallas_call | solution.py:393
  37.8 0.0 copy-start.2
  37.8 0.0 copy-start.1
  37.8 2.8 %copy.14 = bf16[4,196,768]{2,0,1:T(4,128)(2,1)} copy(bf16[4,196,768]{2,0,1:T(4,128)(2,1)} %bitcast.5) | data formatting | bytes 2408448
  40.6 0.0 copy-done.2
  40.6 0.0 copy-start
  40.6 0.6 %copy.15 = f32[768,16]{0,1:T(8,128)} copy(f32[768,16]{0,1:T(8,128)S(1)} %bitcast.8) | data formatting | bytes 98304
  41.2 0.0 copy-done.1
  41.2 1.0 %copy.16 = bf16[1,384,1536]{2,1,0:T(8,128)(2,1)} copy(bf16[1,384,1536]{2,1,0:T(8,128)(2,1)S(1)} %copy-done.1) | data formatting | bytes 2359296
  42.2 0.0 copy-done
  42.2 1.0 %copy.17 = bf16[1,1536,384]{2,1,0:T(8,128)(2,1)} copy(bf16[1,1536,384]{2,1,0:T(8,128)(2,1)S(1)} %copy-done) | data formatting | bytes 2359296
Async XLA Ops:
  37.8 2.8 %copy-start.2 = (f32[16,768]{1,0:T(8,128)S(1)}, f32[16,768]{1,0:T(8,128)}, u32[]{:S(2)}) copy-start(f32[16,768]{1,0:T(8,128)} %get-tuple-element.9) | copy-start | bytes 147460
  37.8 3.4 %copy-start.1 = (bf16[1,384,1536]{2,1,0:T(8,128)(2,1)S(1)}, bf16[1,384,1536]{2,1,0:T(8,128)(2,1)}, u32[]{:S(2)}) copy-start(bf16[1,384,1536]{2,1,0:T(8,128)(2,1)} %get-tuple-element.18) | copy-start | bytes 3538948
  40.6 1.6 %copy-start = (bf16[1,1536,384]{2,1,0:T(8,128)(2,1)S(1)}, bf16[1,1536,384]{2,1,0:T(8,128)(2,1)}, u32[]{:S(2)}) copy-start(bf16[1,1536,384]{2,1,0:T(8,128)(2,1)} %get-tuple-element.19) | copy-start | bytes 3538948

commit v3 on v2

--- a/solution.py
+++ b/solution.py
@@ -16,6 +16,11 @@
 TN = (((0,), (0,)), ((), ()))
 
 
+HOLD = pltpu.VMEM
+LIMIT = 56 << 20
+TAIL_LIMIT = 16 << 20
+
+
 def mm(a, b, dims):
     return lax.dot_general(a, b, dims, preferred_element_type=F32)
 
@@ -30,10 +35,10 @@
 def kernel(
     n_e, n_p, n_d,
     tok_hbm, phi_ref, win_hbm, wout_hbm, so_hbm, go_hbm,
-    tg_hbm, phit_ref, gw1_hbm, gw2_hbm,
-    tok3, go3, tok, go, so, win, wout, disp, comb, low, sp, zg, recv, act, dpre,
-    back, bin_, ret, sigr, phi_acc, ps, pr, qb, fin, tg, gw1, gw2,
-    in_sem, w_sem, out_sem,
+    low, sp, phit_ref, gw1, gw2,
+    tok3, go3, tok, go, so, win, wout, disp, comb, zg, recv, act, dpre,
+    back, bin_, ret, sigr, phi_acc, ps, pr, qb, fin,
+    in_sem, w_sem,
     a_send, a_recv, y_send, y_recv, c_send, c_recv, c2_send, c2_recv,
     b_send, b_recv, r_send, r_recv, p_send, p_recv, q_send, q_recv, f_send, f_recv, own_sem,
 ):
@@ -47,6 +52,8 @@
     hidden = win.shape[1]
     fc = chunk_of(hidden)
     half = width // n_d
+    n_lo, n_hi = fin.shape[0], qb.shape[0]
+    e_hi, e_lo = e // n_lo, e % n_lo
 
     def dev(ee, pp, dd):
         return {"expert": ee, "pair": pp, "dp": dd}
@@ -69,6 +76,9 @@
     barrier = pltpu.get_barrier_semaphore()
     peers = [dev(e_at[k], p, d) for k in range(1, n_e)]
     peers += [dev(e, p_at[i], d_at[j]) for i in range(n_p) for j in range(n_d) if i or j]
+    lo_at = [e_hi * n_lo + rem(e_lo + k, n_lo) for k in range(n_lo)]
+    plane = [(a, i, j) for a in range(n_lo) for i in range(n_p) for j in range(n_d) if a or i or j]
+    peers += [dev(lo_at[a], p_at[i], d_at[j]) for a, i, j in plane if a and (i or j)]
     for peer in peers:
         pl.semaphore_signal(barrier, inc=1, device_id=peer, device_id_type=MESH)
 
@@ -256,8 +266,6 @@
         return carry
 
     lax.fori_loop(0, hidden // fc, grads_in, 0)
-    outs = [pltpu.make_async_copy(gw1, gw1_hbm.at[0], out_sem.at[0])]
-    outs[0].start()
 
     for k in range(1, n_e):
         blk = sigr.at[e_from[k]]
@@ -268,72 +276,85 @@
     dm = disp[...]
     lg_low = (dm * (dg - jnp.sum(dm * dg, axis=1, keepdims=True)) + comb[...]).astype(BF16)
     phi_acc[...] = mm(lg_low, tok[...], NN)
+    per = ps.shape[3]
     for k in range(n_e):
         piece = None
         for b in range(images):
             term = phi_acc[pl.ds(k * rows + b * slots, slots), :]
             piece = term if piece is None else piece + term
-        ps[k] = piece
+        at, off = (k * slots) // per, (k * slots) % per
+        ps[at // (n_p * n_d), (at // n_d) % n_p, at % n_d, pl.ds(off, slots), :] = piece
+
+    def lo_from(k):
+        return rem(e_lo + n_lo - k, n_lo)
+
     out_p = []
-    for k in range(1, n_e):
-        cp = rcopy(ps.at[e_at[k]], pr.at[e], p_send.at[k], p_recv.at[k], dev(e_at[k], p, d))
+    for a, i, j in plane:
+        cp = rcopy(
+            ps.at[rem(e_lo + a, n_lo), p_at[i], d_at[j]], pr.at[e_lo, p, d],
+            p_send.at[a, i, j], p_recv.at[a, i, j], dev(lo_at[a], p_at[i], d_at[j]),
+        )
         cp.start()
         out_p.append(cp)
-    pr[e] = ps[e]
+    pr[e_lo, p, d] = ps[e_lo, p, d]
 
     low[pl.ds(total, total), :] = lg_low
     sp[pl.ds(0, total), :] = sig
-    tg[...] = mm(low[...], sp[...], TN).astype(BF16).reshape(toks, images, width)
-    cp = pltpu.make_async_copy(tg, tg_hbm, out_sem.at[2])
-    cp.start()
-    outs.append(cp)
-
-    for k in range(1, n_e):
-        blk = pr.at[e_from[k]]
-        rcopy(blk, blk, p_send.at[k], p_recv.at[k], dev(e, p, d)).wait_recv()
-    qb[d, p] = jnp.sum(pr[...], axis=0)
+    lax.fori_loop(0, hidden // fc, grads_out, 0)
+
+    for a, i, j in plane:
+        blk = pr.at[lo_from(a), p_from[i], d_from[j]]
+        rcopy(blk, blk, p_send.at[a, i, j], p_recv.at[a, i, j], dev(e, p, d)).wait_recv()
+    qb[e_hi] = jnp.sum(pr[...], axis=(0, 1, 2))
     out_q = []
-    for j in range(n_d):
-        for i in range(n_p):
-            if i or j:
-                cp = rcopy(
-                    qb.at[d, p], qb.at[d, p], q_send.at[j, i], q_recv.at[j, i], dev(e, p_at[i], d_at[j])
-                )
-                cp.start()
-                out_q.append(cp)
-
-    lax.fori_loop(0, hidden // fc, grads_out, 0)
-    cp = pltpu.make_async_copy(gw2, gw2_hbm.at[0], out_sem.at[1])
-    cp.start()
-    outs.append(cp)
-
-    for j in range(n_d):
-        for i in range(n_p):
-            if i or j:
-                blk = qb.at[d_from[j], p_from[i]]
-                rcopy(blk, blk, q_send.at[j, i], q_recv.at[j, i], dev(e, p, d)).wait_recv()
-    whole = None
-    for j in range(n_d):
-        for i in range(n_p):
-            whole = qb[j, i] if whole is None else whole + qb[j, i]
-    fin[e] = whole
-    out_f = []
-    for k in range(1, n_e):
-        cp = rcopy(fin.at[e], fin.at[e], f_send.at[k], f_recv.at[k], dev(e_at[k], p, d))
-        cp.start()
-        out_f.append(cp)
-    for group in (out_a, out_y, out_c, out_c2, out_b, out_r, out_p, out_q):
+    for k in range(1, n_hi):
+        to = rem(e + k * n_lo, n_e)
+        cp = rcopy(qb.at[e_hi], qb.at[e_hi], q_send.at[k], q_recv.at[k], dev(to, p, d))
+        cp.start()
+        out_q.append(cp)
+    for group in (out_a, out_y, out_c, out_c2, out_b, out_r, out_p):
         for cp in group:
             cp.wait_send()
+    for k in range(1, n_hi):
+        blk = qb.at[rem(e_hi + n_hi - k, n_hi)]
+        rcopy(blk, blk, q_send.at[k], q_recv.at[k], dev(e, p, d)).wait_recv()
+    fin[e_lo, p, d] = jnp.sum(qb[...], axis=0)
+    out_f = []
+    for a, i, j in plane:
+        mine = fin.at[e_lo, p, d]
+        cp = rcopy(mine, mine, f_send.at[a, i, j], f_recv.at[a, i, j], dev(lo_at[a], p_at[i], d_at[j]))
+        cp.start()
+        out_f.append(cp)
+    for cp in out_q:
+        cp.wait_send()
+    for a, i, j in plane:
+        blk = fin.at[lo_from(a), p_from[i], d_from[j]]
+        rcopy(blk, blk, f_send.at[a, i, j], f_recv.at[a, i, j], dev(e, p, d)).wait_recv()
+    for at in range(n_lo * n_p * n_d):
+        phit_ref[pl.ds(at * per, per), :] = fin[at // (n_p * n_d), (at // n_d) % n_p, at % n_d]
+    for cp in out_f:
+        cp.wait_send()
+
+
+def finish(low, sp, phi_ref, gw1, gw2, tg_hbm, phi_out, gw1_hbm, gw2_hbm, tg, sem):
+    toks, images, width = tg.shape
+    outs = [
+        pltpu.make_async_copy(gw1, gw1_hbm.at[0], sem.at[0]),
+        pltpu.make_async_copy(gw2, gw2_hbm.at[0], sem.at[1]),
+    ]
+    for cp in outs:
+        cp.start()
+    phi_out[...] = phi_ref[...]
+    low_t = low[...].T
+    part = width // 2 if width % 256 == 0 else width
+    for c in range(width // part):
+        cols = pl.ds(c * part, part)
+        tg[:, :, cols] = mm(low_t, sp[:, cols], NN).astype(BF16).reshape(toks, images, part)
+        cp = pltpu.make_async_copy(tg.at[:, :, cols], tg_hbm.at[:, :, cols], sem.at[2 + c])
+        cp.start()
+        outs.append(cp)
     for cp in outs:
         cp.wait()
-    for k in range(1, n_e):
-        blk = fin.at[e_from[k]]
-        rcopy(blk, blk, f_send.at[k], f_recv.at[k], dev(e, p, d)).wait_recv()
-    for k in range(n_e):
-        phit_ref[pl.ds(k * slots, slots), :] = fin[k]
-    for cp in out_f:
-        cp.wait_send()
 
 
 def local(n_e, n_p, n_d, tokens, phi, w_in, w_out, slot_out, grad_out):
@@ -344,8 +365,12 @@
     rows = images * slots
     half = width // n_d
     group = n_p * n_e * rows
+    n_lo = 2 if n_e % 2 == 0 else 1
+    per = slots_all // (n_lo * n_p * n_d)
+    total = images * slots_all
     vm = pltpu.VMEM
     sem = pltpu.SemaphoreType.DMA
+    pieces = (n_lo, n_p, n_d, per, width)
     scratch = [
         vm((toks, images, width), BF16),
         vm((toks, images, width), BF16),
@@ -354,10 +379,8 @@
         vm((images, slots_all, width), BF16),
         vm((width, hidden), BF16),
         vm((hidden, width), BF16),
-        vm((images * slots_all, toks * images), F32),
-        vm((images * slots_all, toks * images), F32),
-        vm((2 * images * slots_all, toks * images), BF16),
-        vm((2 * images * slots_all, width), BF16),
+        vm((total, toks * images), F32),
+        vm((total, toks * images), F32),
         vm((2, n_e, rows, width), BF16),
         vm((2, n_d, n_p, n_e, rows, width), BF16),
         vm((n_d, group, hidden), BF16),
@@ -366,16 +389,12 @@
         vm((n_p - 1, n_e * rows, width), F32),
         vm((n_e, rows, width), BF16),
         vm((n_e, rows, width), BF16),
-        vm((images * slots_all, width), F32),
-        vm((n_e, slots, width), F32),
-        vm((n_e, slots, width), F32),
-        vm((n_d, n_p, slots, width), F32),
-        vm((n_e, slots, width), F32),
-        vm((toks, images, width), BF16),
-        vm((half, hidden), BF16),
-        vm((hidden, half), BF16),
+        vm((total, width), F32),
+        vm(pieces, F32),
+        vm(pieces, F32),
+        vm((n_e // n_lo, per, width), F32),
+        vm(pieces, F32),
         sem((2,)),
-        sem((3,)),
         sem((3,)),
     ]
     scratch += [sem((n_e,))] * 2
@@ -384,27 +403,43 @@
     scratch += [sem((n_d, n_p, n_e))] * 2
     scratch += [sem((n_p,))] * 2
     scratch += [sem((n_e,))] * 2
-    scratch += [sem((n_e,))] * 2
-    scratch += [sem((n_d, n_p))] * 2
-    scratch += [sem((n_e,))] * 2
+    scratch += [sem((n_lo, n_p, n_d))] * 2
+    scratch += [sem((n_e // n_lo,))] * 2
+    scratch += [sem((n_lo, n_p, n_d))] * 2
     scratch += [sem((1,))]
     hbm = pl.BlockSpec(memory_space=pl.ANY)
     vmem = pl.BlockSpec(memory_space=pltpu.VMEM)
-    token_grad, phi_t, gw1, gw2 = pl.pallas_call(
+    struct = jax.ShapeDtypeStruct
+    passed = pl.pallas_call(
         functools.partial(kernel, n_e, n_p, n_d),
-        out_shape=(
-            jax.ShapeDtypeStruct((toks, images, width), BF16),
-            jax.ShapeDtypeStruct((slots_all, width), F32),
-            jax.ShapeDtypeStruct((1, half, hidden), BF16),
-            jax.ShapeDtypeStruct((1, hidden, half), BF16),
+        out_shape=tuple(
+            HOLD(shape, dtype)
+            for shape, dtype in (
+                ((2 * total, toks * images), BF16),
+                ((2 * total, width), BF16),
+                ((slots_all, width), F32),
+                ((half, hidden), BF16),
+                ((hidden, half), BF16),
+            )
         ),
         in_specs=[hbm, vmem, hbm, hbm, hbm, hbm],
+        out_specs=(vmem,) * 5,
+        scratch_shapes=scratch,
+        compiler_params=pltpu.CompilerParams(collective_id=0, has_side_effects=True, vmem_limit_bytes=LIMIT),
+    )(jnp.transpose(tokens, (1, 0, 2)), phi.T, w_in, w_out, slot_out, jnp.transpose(grad_out, (1, 0, 2)))
+    token_grad, phi_t, gw1, gw2 = pl.pallas_call(
+        finish,
+        out_shape=(
+            struct((toks, images, width), BF16),
+            struct((slots_all, width), F32),
+            struct((1, half, hidden), BF16),
+            struct((1, hidden, half), BF16),
+        ),
+        in_specs=[vmem] * 5,
         out_specs=(hbm, vmem, hbm, hbm),
-        scratch_shapes=scratch,
-        compiler_params=pltpu.CompilerParams(collective_id=0, has_side_effects=True),
-    )(
-        jnp.transpose(tokens, (1, 0, 2)), phi.T, w_in, w_out, slot_out, jnp.transpose(grad_out, (1, 0, 2))
-    )
+        scratch_shapes=[vm((toks, images, width), BF16), sem((4,))],
+        compiler_params=pltpu.CompilerParams(vmem_limit_bytes=TAIL_LIMIT),
+    )(*(pltpu.with_memory_space_constraint(x, pltpu.VMEM) for x in passed))
     return (jnp.transpose(token_grad, (1, 0, 2)), phi_t.T, gw1, gw2)
 
 

time: 43.4 us -> 38.8 us (0.89)
  local copies, waits for them, and re-layouts: 5.47 us -> 0 us
  Pallas kernels: 37.1 us -> 38 us
    unnamed x10 -> x0, local copies, waits for them, and re-layouts: 5.47 us -> none
    pallas_call x1 -> x2, Pallas kernels: 37.1 us -> 38 us  [the longest x1 35.5 us: local(): pl.pallas_call(functools.partial(kernel, n_e, n_p, n_d), out_shape=tuple(...]
where the time goes in v3:
time: 38.8 us; the launch traced here: 38.6 us
  Pallas kernels  38 us (98%)
  between operations  0.64 us (2%)
    pallas_call x1, Pallas kernels, local(): pl.pallas_call(functools.partial(kernel, n_e, n_p, n_d), out_shape=tuple(...  35.5 us
    pallas_call x1, Pallas kernels, local(): pl.pallas_call(finish, out_shape=(struct((toks, images, width), BF16), st...  2.49 us

profile of v3, /device:TPU:0, one launch (start us, length us, event | category | flops | bytes accessed | tf_op | source)
XLA Modules:
  0.0 38.6 jit_solution(16572769820518485366)
XLA Ops:
  0.6 35.5 %shard_map.93 = (bf16[128,784]{1,0:T(8,128)(2,1)S(1)}, bf16[128,768]{1,0:T(8,128)(2,1)S(1)}, f32[16,768]{1,0:T(8,128)S(1)}, bf16[384,1536]{1,0:T(8,128)(2,1)S(1)}, bf16[1536,384]{1,0:T(8,128)(2,1)S(1)}) custom-call(bf16[196,4,768]{2,1,0:T(4,128)(2,1)} %bitcast.5, bf16[16,768]{1,0:T(8,128)(2,1)} %bitcast.7, bf16[1,768,1536]{2,1,0:T(8,128)(2,1)} %win_hbm.1, ...), custom_call_target="tpu_custom_call" | custom-call | tf_op jit(solution)/shard_map/pallas_call | solution.py:413
  36.1 2.5 %shard_map.94 = (bf16[196,4,768]{2,1,0:T(4,128)(2,1)}, f32[16,768]{1,0:T(8,128)}, bf16[1,384,1536]{2,1,0:T(8,128)(2,1)}, bf16[1,1536,384]{2,1,0:T(8,128)(2,1)}) custom-call(bf16[128,784]{1,0:T(8,128)(2,1)S(1)} %get-tuple-element.13.low, bf16[128,768]{1,0:T(8,128)(2,1)S(1)} %get-tuple-element.14.sp, f32[16,768]{1,0:T(8,128)S(1)} %get-tuple-element.15.phi_ref, ...), custom_call_target="tpu_custom_call" | custom-call | tf_op jit(solution)/shard_map/pallas_call | solution.py:430

commit v4 on v3

--- a/solution.py
+++ b/solution.py
@@ -35,8 +35,8 @@
 def kernel(
     n_e, n_p, n_d,
     tok_hbm, phi_ref, win_hbm, wout_hbm, so_hbm, go_hbm,
-    low, sp, phit_ref, gw1, gw2,
-    tok3, go3, tok, go, so, win, wout, disp, comb, zg, recv, act, dpre,
+    tg, phit_ref, gw1, gw2,
+    low, sp, tok3, go3, tok, go, so, win, wout, disp, comb, zg, recv, act, dpre,
     back, bin_, ret, sigr, phi_acc, ps, pr, qb, fin,
     in_sem, w_sem,
     a_send, a_recv, y_send, y_recv, c_send, c_recv, c2_send, c2_recv,
@@ -124,6 +124,16 @@
     disp[...] = by_tok
     low[pl.ds(0, total), :] = by_tok.astype(BF16)
     zg[0] = mm(by_tok.astype(BF16), tok[...], NN).astype(BF16).reshape(n_e, rows, width)
+    pl.semaphore_wait(barrier, len(peers))
+
+    out_a = []
+    for k in range(1, n_e):
+        cp = rcopy(
+            zg.at[0, e_at[k]], recv.at[0, d, p, e],
+            a_send.at[0, k], a_recv.at[0, k], dev(e_at[k], p, d),
+        )
+        cp.start()
+        out_a.append(cp)
     by_slot = jnp.exp(logits - jnp.max(logits, axis=0, keepdims=True))
     by_slot = by_slot / jnp.sum(by_slot, axis=0, keepdims=True)
     comb[...] = by_slot
@@ -131,12 +141,10 @@
     go[...] = go3[...].reshape(lanes, width)
     zg[1] = mm(by_slot.astype(BF16), go[...], NN).astype(BF16).reshape(n_e, rows, width)
 
-    pl.semaphore_wait(barrier, len(peers))
-
-    out_a = []
     for k in range(1, n_e):
         cp = rcopy(
-            zg.at[:, e_at[k]], recv.at[:, d, p, e], a_send.at[k], a_recv.at[k], dev(e_at[k], p, d)
+            zg.at[1, e_at[k]], recv.at[1, d, p, e],
+            a_send.at[1, k], a_recv.at[1, k], dev(e_at[k], p, d),
         )
         cp.start()
         out_a.append(cp)
@@ -157,7 +165,9 @@
         if k == 0:
             own.wait()
         else:
-            rcopy(blk, blk, a_send.at[k], a_recv.at[k], dev(e, p, d)).wait_recv()
+            for w in range(2):
+                half_blk = recv.at[w, d, p, e_from[k]]
+                rcopy(half_blk, half_blk, a_send.at[w, k], a_recv.at[w, k], dev(e, p, d)).wait_recv()
         for i in range(1, n_p):
             cp = rcopy(blk, blk, c_send.at[i, k], c_recv.at[i, k], dev(e, p_at[i], d))
             cp.start()
@@ -215,6 +225,18 @@
         cp.start()
         out_b.append(cp)
 
+    acc = back[p]
+    for i in range(1, n_p):
+        rcopy(bin_.at[i - 1], bin_.at[i - 1], b_send.at[i], b_recv.at[i], dev(e, p, d)).wait_recv()
+        acc = acc + bin_[i - 1]
+    ret[...] = acc.astype(BF16).reshape(n_e, rows, width)
+    out_r = []
+    for k in range(1, n_e):
+        cp = rcopy(ret.at[e_at[k]], sigr.at[e], r_send.at[k], r_recv.at[k], dev(e_at[k], p, d))
+        cp.start()
+        out_r.append(cp)
+    sigr[e] = ret[e]
+
     for j in range(1, n_d):
         for k in range(n_e):
             blk = recv.at[:, d_from[j], p, e_from[k]]
@@ -223,18 +245,6 @@
                 cp = rcopy(blk, blk, c2_send.at[j, i, k], c2_recv.at[j, i, k], dev(e, p_at[i], d))
                 cp.start()
                 out_c2.append(cp)
-
-    acc = back[p]
-    for i in range(1, n_p):
-        rcopy(bin_.at[i - 1], bin_.at[i - 1], b_send.at[i], b_recv.at[i], dev(e, p, d)).wait_recv()
-        acc = acc + bin_[i - 1]
-    ret[...] = acc.astype(BF16).reshape(n_e, rows, width)
-    out_r = []
-    for k in range(1, n_e):
-        cp = rcopy(ret.at[e_at[k]], sigr.at[e], r_send.at[k], r_recv.at[k], dev(e_at[k], p, d))
-        cp.start()
-        out_r.append(cp)
-    sigr[e] = ret[e]
 
     for j in range(1, n_d):
         for i in range(1, n_p):
@@ -315,6 +325,7 @@
     for group in (out_a, out_y, out_c, out_c2, out_b, out_r, out_p):
         for cp in group:
             cp.wait_send()
+    tg[...] = mm(low[...], sp[...], TN).astype(BF16).reshape(toks, images, width)
     for k in range(1, n_hi):
         blk = qb.at[rem(e_hi + n_hi - k, n_hi)]
         rcopy(blk, blk, q_send.at[k], q_recv.at[k], dev(e, p, d)).wait_recv()
@@ -336,23 +347,17 @@
         cp.wait_send()
 
 
-def finish(low, sp, phi_ref, gw1, gw2, tg_hbm, phi_out, gw1_hbm, gw2_hbm, tg, sem):
-    toks, images, width = tg.shape
+def finish(tg, phi_ref, gw1, gw2, tg_hbm, phi_out, gw1_hbm, gw2_hbm, sem):
+    cut = tg.shape[0] // 2
     outs = [
-        pltpu.make_async_copy(gw1, gw1_hbm.at[0], sem.at[0]),
-        pltpu.make_async_copy(gw2, gw2_hbm.at[0], sem.at[1]),
+        pltpu.make_async_copy(tg.at[:cut], tg_hbm.at[:cut], sem.at[0]),
+        pltpu.make_async_copy(tg.at[cut:], tg_hbm.at[cut:], sem.at[1]),
+        pltpu.make_async_copy(gw1, gw1_hbm.at[0], sem.at[2]),
+        pltpu.make_async_copy(gw2, gw2_hbm.at[0], sem.at[3]),
     ]
     for cp in outs:
         cp.start()
     phi_out[...] = phi_ref[...]
-    low_t = low[...].T
-    part = width // 2 if width % 256 == 0 else width
-    for c in range(width // part):
-        cols = pl.ds(c * part, part)
-        tg[:, :, cols] = mm(low_t, sp[:, cols], NN).astype(BF16).reshape(toks, images, part)
-        cp = pltpu.make_async_copy(tg.at[:, :, cols], tg_hbm.at[:, :, cols], sem.at[2 + c])
-        cp.start()
-        outs.append(cp)
     for cp in outs:
         cp.wait()
 
@@ -372,6 +377,8 @@
     sem = pltpu.SemaphoreType.DMA
     pieces = (n_lo, n_p, n_d, per, width)
     scratch = [
+        vm((2 * total, toks * images), BF16),
+        vm((2 * total, width), BF16),
         vm((toks, images, width), BF16),
         vm((toks, images, width), BF16),
         vm((toks * images, width), BF16),
@@ -397,7 +404,7 @@
         sem((2,)),
         sem((3,)),
     ]
-    scratch += [sem((n_e,))] * 2
+    scratch += [sem((2, n_e))] * 2
     scratch += [sem((n_d, n_e))] * 2
     scratch += [sem((n_p, n_e))] * 2
     scratch += [sem((n_d, n_p, n_e))] * 2
@@ -415,15 +422,14 @@
         out_shape=tuple(
             HOLD(shape, dtype)
             for shape, dtype in (
-                ((2 * total, toks * images), BF16),
-                ((2 * total, width), BF16),
+                ((toks, images, width), BF16),
                 ((slots_all, width), F32),
                 ((half, hidden), BF16),
                 ((hidden, half), BF16),
             )
         ),
         in_specs=[hbm, vmem, hbm, hbm, hbm, hbm],
-        out_specs=(vmem,) * 5,
+        out_specs=(vmem,) * 4,
         scratch_shapes=scratch,
         compiler_params=pltpu.CompilerParams(collective_id=0, has_side_effects=True, vmem_limit_bytes=LIMIT),
     )(jnp.transpose(tokens, (1, 0, 2)), phi.T, w_in, w_out, slot_out, jnp.transpose(grad_out, (1, 0, 2)))
@@ -435,9 +441,9 @@
             struct((1, half, hidden), BF16),
             struct((1, hidden, half), BF16),
         ),
-        in_specs=[vmem] * 5,
+        in_specs=[vmem] * 4,
         out_specs=(hbm, vmem, hbm, hbm),
-        scratch_shapes=[vm((toks, images, width), BF16), sem((4,))],
+        scratch_shapes=[sem((4,))],
         compiler_params=pltpu.CompilerParams(vmem_limit_bytes=TAIL_LIMIT),
     )(*(pltpu.with_memory_space_constraint(x, pltpu.VMEM) for x in passed))
     return (jnp.transpose(token_grad, (1, 0, 2)), phi_t.T, gw1, gw2)

time: 38.8 us -> 38.7 us (level)
  no operation moved by 1% of the time
where the time goes in v4:
time: 38.7 us; the launch traced here: 38.5 us
  Pallas kernels  37.9 us (98%)
  between operations  0.64 us (2%)
    pallas_call x1, Pallas kernels, local(): pl.pallas_call(functools.partial(kernel, n_e, n_p, n_d), out_shape=tuple(...  35.4 us
    pallas_call x1, Pallas kernels, local(): pl.pallas_call(finish, out_shape=(struct((toks, images, width), BF16), st...  2.46 us

profile of v4, /device:TPU:0, one launch (start us, length us, event | category | flops | bytes accessed | tf_op | source)
XLA Modules:
  0.0 38.5 jit_solution(7359827314376006252)
XLA Ops:
  0.6 35.4 %shard_map.93 = (bf16[196,4,768]{2,1,0:T(4,128)(2,1)S(1)}, f32[16,768]{1,0:T(8,128)S(1)}, bf16[384,1536]{1,0:T(8,128)(2,1)S(1)}, bf16[1536,384]{1,0:T(8,128)(2,1)S(1)}) custom-call(bf16[196,4,768]{2,1,0:T(4,128)(2,1)} %bitcast.5, bf16[16,768]{1,0:T(8,128)(2,1)} %bitcast.7, bf16[1,768,1536]{2,1,0:T(8,128)(2,1)} %win_hbm.1, bf16[1,1536,768]{2,1,0:T(8,128)(2,1)} %wout_hbm.1, ...), custom_call_target="tpu_custom_call" | custom-call | tf_op jit(solution)/shard_map/pallas_call | solution.py:420
  36.0 2.5 %shard_map.94 = (bf16[196,4,768]{2,1,0:T(4,128)(2,1)}, f32[16,768]{1,0:T(8,128)}, bf16[1,384,1536]{2,1,0:T(8,128)(2,1)}, bf16[1,1536,384]{2,1,0:T(8,128)(2,1)}) custom-call(bf16[196,4,768]{2,1,0:T(4,128)(2,1)S(1)} %get-tuple-element.12.tg, f32[16,768]{1,0:T(8,128)S(1)} %get-tuple-element.13.phi_ref, bf16[384,1536]{1,0:T(8,128)(2,1)S(1)} %get-tuple-element.14.gw1, ...), custom_call_target="tpu_custom_call" | custom-call | tf_op jit(solution)/shard_map/pallas_call | solution.py:436
